TPU v7x, 512 devices: a whole 4x8x8 slice. The times are simulated.
512 devices in a mesh: pts: 128 (over x, z, y_lo, core), lmk: 4 (over y_hi).
Axes of the slice: x: 4, y: 8 (y_hi: 4, y_lo: 2; y = y_hi * 2 + y_lo), z: 8, core: 2. Of those that a mesh axis runs over, the one named last changes fastest.
Arguments:
- points: bfloat16 [32768, 768], P('pts'), may hold values from -6 to 6
- landmarks: bfloat16 [384, 768], P('lmk'), may hold values from -6 to 6
- panels: bfloat16 [128, 384, 2048], P('pts', None, 'lmk'), may hold values from -0.3125 to 0.3125
- panel_index: int32 [1], replicated, may hold values from 0 to 127
- assignment: int32 [32768], P('pts'), may hold values from 0 to 4095, as said below
Outputs:
- centroid_sums: float32 [4096, 2048], P('pts', 'lmk')
- cluster_counts: int32 [4096], P('pts')
Inputs may be any that keep to these rules, and one draw needn't show every extreme that they name: `assignment`: owner of a cluster c is c // 32. In each aligned block of 256 points (the points of one device) at most 4 points have clusters of one owner; one owner, the same for every block, has exactly 4 points in every block.
All inputs are finite; a program needn't handle non-finite values.
Results may differ from a plain program's by a relative error of at most 0.0017.
Values may be sent and summed in bfloat16 or wider, within the bound.
A program may use at most 64 MiB of HBM per device.

v0:
```python
import math
import jax
import jax.numpy as jnp
from jax import lax
from jax.sharding import PartitionSpec as P

CLUSTERS = 4096


def spread(block, axis, holder):
    block = jnp.where(lax.axis_index(axis) == holder, block, jnp.zeros_like(block))
    return lax.psum(block, axis)


def unit_rows(values_in):
    widened = values_in.astype(jnp.float32)
    scale = lax.rsqrt(jnp.mean(widened * widened, axis=1, keepdims=True) + 1e-06)
    return (widened * scale).astype(jnp.bfloat16)


def kernel_rows(unit_points, unit_marks):
    scores = lax.dot_general(
        unit_points, unit_marks, (((1,), (1,)), ((), ())), preferred_element_type=jnp.float32
    )
    return jnp.exp(scores * (0.5 / math.sqrt(unit_points.shape[1]))).astype(jnp.bfloat16)


def body(points, landmarks, panels, panel_index, assignment):
    point_groups = lax.axis_size("pts")
    point_rows = points.shape[0]
    unit_points = unit_rows(points)
    kernel = kernel_rows(
        unit_points, unit_rows(lax.all_gather(landmarks, "lmk", axis=0, tiled=True))
    )
    factor_panel = spread(panels[0], "pts", panel_index[0])
    owned_clusters = CLUSTERS // point_groups
    capacity = 2 * point_rows // point_groups
    owners = assignment // owned_clusters
    local_id = assignment - owners * owned_clusters
    owner_hits = (owners[:, None] == jnp.arange(point_groups, dtype=jnp.int32)[None, :]).astype(
        jnp.int32
    )
    slot_rank = jnp.sum(jnp.cumsum(owner_hits, axis=0) * owner_hits, axis=1) - 1
    slot_ids = jnp.full((point_groups, capacity), -1, jnp.int32).at[owners, slot_rank].set(local_id)
    features = jnp.dot(kernel, factor_panel, preferred_element_type=jnp.float32).astype(
        jnp.bfloat16
    )
    slots = (
        jnp.zeros((point_groups, capacity, features.shape[1]), jnp.bfloat16)
        .at[owners, slot_rank]
        .set(features)
    )
    arrived, arrived_ids = (
        lax.all_to_all(slots, "pts", split_axis=0, concat_axis=0, tiled=True),
        lax.all_to_all(slot_ids, "pts", split_axis=0, concat_axis=0, tiled=True),
    )
    received = arrived.reshape(-1, arrived.shape[2])
    membership = (
        arrived_ids.reshape(-1)[None, :] == jnp.arange(owned_clusters, dtype=jnp.int32)[:, None]
    )
    totals = jnp.dot(membership.astype(jnp.bfloat16), received, preferred_element_type=jnp.float32)
    counts = jnp.sum(membership.astype(jnp.int32), axis=1)
    mean_count = point_rows * point_groups / CLUSTERS
    return (totals / mean_count, counts)


def solution(mesh):
    in_specs = (P("pts", None), P("lmk", None), P("pts", None, "lmk"), P(), P("pts"))
    out_specs = (P("pts", "lmk"), P("pts"))
    return jax.shard_map(body, mesh=mesh, in_specs=in_specs, out_specs=out_specs, check_vma=False)
```

profile of v0, /device:TPU:1, one launch (start us, length us, event | category | flops | bytes accessed | tf_op | source)
XLA Modules:
  0.0 1064.7 jit_solution(14033932260171003460)
XLA Ops:
  7.2 0.0 all-reduce.2.cloned.1.call-start
  7.9 0.0 copy-start.2
  7.9 0.8 select_bitcast_fusion
  8.7 0.0 all-reduce.2.cloned.1.call-update
  8.7 0.0 copy-done.2
  8.7 0.1 copy.13
  8.8 0.2 fusion.15
  9.1 0.2 fusion.16
  9.4 0.0 copy-start
  9.4 11.1 %scatter_fusion = s32[128,4]{0,1:T(4,128)S(1)} fusion(s32[128,4]{0,1:T(4,128)S(1)} %broadcast_in_dim.8, s32[256]{0:T(256)S(1)} %bitcast.24, s32[256]{0:T(256)S(1)} %get-tuple-element.2), kind=kCustom, calls=%fused_computation | custom fusion | bytes 5120 | tf_op jit(solution)/shard_map/scatter | solution.py:44
  20.4 0.0 copy-start.1
  20.5 0.7 copy.15
  21.2 16.6 %all-to-all-start = ((s32[128,1,4]{2,1,0:T(1,128)}), s32[128,1,4]{2,1,0:T(1,128)S(1)}, u32[]{:S(2)}, u32[]{:S(2)}) async-start(s32[128,1,4]{2,1,0:T(1,128)} %copy.15), calls=%async_computation | async-start | bytes 131072 | tf_op jit(solution)/shard_map/all_to_all | solution.py:55
  37.8 0.0 copy-done
  37.8 0.2 fusion.4
  38.0 0.0 copy-done.1
  38.0 15.6 %all_gather.3 = bf16[384,768]{1,0:T(8,128)(2,1)S(1)} all-gather(bf16[96,768]{1,0:T(8,128)(2,1)S(1)} %copy-done.1), channel_id=1, replica_groups=mesh['pts'=128,'lmk'=4] {'lmk'}, dimensions={0}, use_global_device_ids=true | all-gather | bytes 737280 | tf_op jit(solution)/shard_map/all_gather | solution.py:33
  53.6 0.2 fusion.1
  53.8 943.7 %all-reduce.2.cloned.1.call-done = bf16[384,512]{1,0:T(8,128)(2,1)} async-done(((bf16[384,512]{1,0:T(8,128)(2,1)}), bf16[384,512]{1,0:T(8,128)(2,1)}) %all-reduce.2.cloned.1.call-update) | async-done | bytes 393232 | tf_op jit(solution)/shard_map/psum | solution.py:12
  997.5 1.7 convolution_convert_fusion
  999.2 0.9 broadcast_in_dim.10
  1000.1 30.6 %scatter_fusion.1 = bf16[128,4,512]{2,1,0:T(4,128)(2,1)} fusion(bf16[128,4,512]{2,1,0:T(4,128)(2,1)} %broadcast_in_dim.10, s32[256]{0:T(256)S(1)} %bitcast.25, bf16[256,512]{1,0:T(8,128)(2,1)S(1)} %convolution_convert_fusion), kind=kCustom, calls=%fused_computation.1 | custom fusion | bytes 788480 | tf_op jit(solution)/shard_map/scatter | solution.py:51
  1030.7 0.0 all-to-all-done
  1030.7 7.8 all-to-all-start.1
  1038.5 0.5 broadcast.135
  1039.0 0.8 reduce.3
  1039.8 0.1 eq.48
  1040.0 0.6 convert_reduce_fusion
  1040.6 16.3 %all-to-all-done.1 = bf16[128,4,512]{2,1,0:T(4,128)(2,1)S(1)} async-done(((bf16[128,4,512]{2,1,0:T(4,128)(2,1)}), bf16[128,4,512]{2,1,0:T(4,128)(2,1)S(1)}, u32[]{:S(2)}, u32[]{:S(2)}) %all-to-all-start.1) | async-done | bytes 524320 | tf_op jit(solution)/shard_map/all_to_all | solution.py:54
  1056.9 0.1 reshape.67
  1057.0 0.8 convolution_multiply_fusion.1
  (13 shorter events, 0.1 us)
Async XLA Ops:
  7.2 990.3 %all-reduce.2.cloned.1.call-start = ((), (), s32[]{:S(2)}) async-start(), calls=%async_computation.2 | async-start | bytes 786432 | tf_op jit(solution)/shard_map/psum | solution.py:12
  7.9 0.8 copy-start.2
  9.4 28.5 %copy-start = (bf16[256,768]{1,0:T(8,128)(2,1)S(1)}, bf16[256,768]{1,0:T(8,128)(2,1)}, u32[]{:S(2)}) copy-start(bf16[256,768]{1,0:T(8,128)(2,1)} %param.5) | copy-start | bytes 1179652
  20.4 17.6 %copy-start.1 = (bf16[96,768]{1,0:T(8,128)(2,1)S(1)}, bf16[96,768]{1,0:T(8,128)(2,1)}, u32[]{:S(2)}) copy-start(bf16[96,768]{1,0:T(8,128)(2,1)} %param.6) | copy-start | bytes 442372
  21.2 1009.5 %all-to-all-start = ((s32[128,1,4]{2,1,0:T(1,128)}), s32[128,1,4]{2,1,0:T(1,128)S(1)}, u32[]{:S(2)}, u32[]{:S(2)}) async-start(s32[128,1,4]{2,1,0:T(1,128)} %copy.15), calls=%async_computation | async-start | bytes 131072 | tf_op jit(solution)/shard_map/all_to_all | solution.py:55
  1030.7 26.2 %all-to-all-start.1 = ((bf16[128,4,512]{2,1,0:T(4,128)(2,1)}), bf16[128,4,512]{2,1,0:T(4,128)(2,1)S(1)}, u32[]{:S(2)}, u32[]{:S(2)}) async-start(bf16[128,4,512]{2,1,0:T(4,128)(2,1)} %scatter_fusion.1), calls=%async_computation.1 | async-start | bytes 1048576 | tf_op jit(solution)/shard_map/all_to_all | solution.py:54
Sparse Core Ops, SparseCore 0:
  10.9 986.5 all-reduce.1
where the time goes:
time: 1070 us; the launch traced here: 1060 us
  waiting for transfers between devices  960 us (90%)
  local copies, waits for them, and re-layouts  44.2 us (4%)
  starting transfers between devices  24.5 us (2%)
  blocking collectives  15.6 us (1%)
  between operations  14.8 us (1%)
    psum x1, waiting for transfers between devices, spread(): return lax.psum(block, axis)  944 us
    scatter x1, local copies, waits for them, and re-layouts, body(): slots = jnp.zeros((point_groups, capacity, features.shape[1]), jnp.bfloat...  30.6 us
  transfers between devices with their start and end apart: 3, of which 2 were waited for; matrix products, arithmetic and copies ran while one was open for 5% of the time, Pallas kernels for 0%

commit v1 on v0

--- a/solution.py
+++ b/solution.py
@@ -9,7 +9,7 @@
 
 def spread(block, axis, holder):
     block = jnp.where(lax.axis_index(axis) == holder, block, jnp.zeros_like(block))
-    return lax.psum(block, axis)
+    return jnp.sum(lax.all_gather(block, axis), axis=0)
 
 
 def unit_rows(values_in):

time: 1070 us -> 398 us (0.37)
  waiting for transfers between devices: 960 us -> 273 us
  other arithmetic: 3.06 us -> 19.4 us
    psum x1 -> x0, waiting for transfers between devices: 944 us -> none  [spread(): return lax.psum(block, axis)]
    all_gather x0 -> x1, waiting for transfers between devices: none -> 257 us  [spread(): return jnp.sum(lax.all_gather(block, axis), axis=0)]
    reduce_sum x0 -> x1, other arithmetic: none -> 16.3 us  [spread(): return jnp.sum(lax.all_gather(block, axis), axis=0)]
  transfers between devices with their start and end apart: 3 -> 3, of which waited for: 2 -> 2; matrix products, arithmetic and copies ran while one was open for 5% -> 16% of each run, Pallas kernels for 0% -> 0%
where the time goes in v1:
time: 398 us; the launch traced here: 397 us
  waiting for transfers between devices  273 us (69%)
  local copies, waits for them, and re-layouts  44.2 us (11%)
  starting transfers between devices  29.1 us (7%)
  other arithmetic  19.4 us (5%)
  between operations  14.9 us (4%)
  blocking collectives  14.8 us (4%)
    all_gather x1, waiting for transfers between devices, spread(): return jnp.sum(lax.all_gather(block, axis), axis=0)  257 us
    scatter x1, local copies, waits for them, and re-layouts, body(): slots = jnp.zeros((point_groups, capacity, features.shape[1]), jnp.bfloat...  30.6 us
    all_to_all x1, starting transfers between devices, body(): lax.all_to_all(slot_ids, 'pts', split_axis=0, concat_axis=0, tiled=True)  16.6 us
    all_to_all x1, waiting for transfers between devices, body(): lax.all_to_all(slots, 'pts', split_axis=0, concat_axis=0, tiled=True)  16.3 us
    reduce_sum x1, other arithmetic, spread(): return jnp.sum(lax.all_gather(block, axis), axis=0)  16.3 us
    all_gather x1, blocking collectives, body(): lax.all_gather(landmarks, 'lmk', axis=0, tiled=True)  14.8 us
    all_to_all x1, starting transfers between devices, body(): lax.all_to_all(slots, 'pts', split_axis=0, concat_axis=0, tiled=True)  12.5 us
    scatter x1, local copies, waits for them, and re-layouts, body(): jnp.full((point_groups, capacity), -1, jnp.int32).at[owners, slot_rank]  11.1 us
  transfers between devices with their start and end apart: 3, of which 2 were waited for; matrix products, arithmetic and copies ran while one was open for 16% of the time, Pallas kernels for 0%

profile of v1, /device:TPU:1, one launch (start us, length us, event | category | flops | bytes accessed | tf_op | source)
XLA Modules:
  0.0 397.0 jit_solution(9809884800264629)
XLA Ops:
  7.2 0.0 copy-start.2
  7.2 0.0 all-gather.2.cloned.1.call-start
  7.9 0.8 broadcast_select_fusion
  8.7 0.0 all-gather.2.cloned.1.call-update
  8.7 0.0 copy-done.2
  8.7 0.1 copy.13
  8.8 0.2 fusion.15
  9.1 0.2 fusion.16
  9.4 0.0 copy-start
  9.4 0.0 copy-start.1
  9.4 11.1 %scatter_fusion = s32[128,4]{0,1:T(4,128)S(1)} fusion(s32[128,4]{0,1:T(4,128)S(1)} %broadcast_in_dim.8, s32[256]{0:T(256)S(1)} %bitcast.24, s32[256]{0:T(256)S(1)} %get-tuple-element.2), kind=kCustom, calls=%fused_computation | custom fusion | bytes 5120 | tf_op jit(solution)/shard_map/scatter | solution.py:44
  20.5 0.7 copy.15
  21.2 16.6 %all-to-all-start = ((s32[128,1,4]{2,1,0:T(1,128)}), s32[128,1,4]{2,1,0:T(1,128)S(1)}, u32[]{:S(2)}, u32[]{:S(2)}) async-start(s32[128,1,4]{2,1,0:T(1,128)} %copy.15), calls=%async_computation | async-start | bytes 131072 | tf_op jit(solution)/shard_map/all_to_all | solution.py:55
  37.8 0.0 copy-done
  37.9 0.2 fusion.4
  38.0 0.0 copy-done.1
  38.0 14.8 %all_gather.7 = bf16[384,768]{1,0:T(8,128)(2,1)S(1)} all-gather(bf16[96,768]{1,0:T(8,128)(2,1)S(1)} %copy-done.1), channel_id=1, replica_groups=mesh['pts'=128,'lmk'=4] {'lmk'}, dimensions={0}, use_global_device_ids=true | all-gather | bytes 737280 | tf_op jit(solution)/shard_map/all_gather | solution.py:33
  52.8 0.2 fusion.1
  53.0 256.8 %all-gather.2.cloned.1.call-done = bf16[128,384,512]{2,1,0:T(8,128)(2,1)} async-done(((bf16[1,384,512]{2,1,0:T(8,128)(2,1)}), bf16[128,384,512]{2,1,0:T(8,128)(2,1)}) %all-gather.2.cloned.1.call-update) | async-done | bytes 50331664 | tf_op jit(solution)/shard_map/all_gather | solution.py:12
  309.8 16.3 %reduce_sum.51 = bf16[384,512]{1,0:T(8,128)(2,1)S(1)} reduce(bf16[128,384,512]{2,1,0:T(8,128)(2,1)} %all-gather.2.cloned.1.call-done, bf16[]{:T(256)} %constant.49.clone.1), dimensions={0}, to_apply=%region_6.7 | reduce | flops 24969216 | bytes 50724864 | tf_op jit(solution)/shard_map/reduce_sum | solution.py:12
  326.1 0.7 convolution_convert_fusion
  326.8 0.9 broadcast_in_dim.10
  327.8 30.6 %scatter_fusion.1 = bf16[128,4,512]{2,1,0:T(4,128)(2,1)} fusion(bf16[128,4,512]{2,1,0:T(4,128)(2,1)} %broadcast_in_dim.10, s32[256]{0:T(256)S(1)} %bitcast.25, bf16[256,512]{1,0:T(8,128)(2,1)S(1)} %convolution_convert_fusion), kind=kCustom, calls=%fused_computation.1 | custom fusion | bytes 788480 | tf_op jit(solution)/shard_map/scatter | solution.py:51
  358.3 0.0 all-to-all-done
  358.3 12.5 %all-to-all-start.1 = ((bf16[128,4,512]{2,1,0:T(4,128)(2,1)}), bf16[128,4,512]{2,1,0:T(4,128)(2,1)S(1)}, u32[]{:S(2)}, u32[]{:S(2)}) async-start(bf16[128,4,512]{2,1,0:T(4,128)(2,1)} %scatter_fusion.1), calls=%async_computation.1 | async-start | bytes 1048576 | tf_op jit(solution)/shard_map/all_to_all | solution.py:54
  370.8 0.5 broadcast.133
  371.3 0.8 reduce.4
  372.1 0.1 eq.48
  372.2 0.6 convert_reduce_fusion
  372.9 16.3 %all-to-all-done.1 = bf16[128,4,512]{2,1,0:T(4,128)(2,1)S(1)} async-done(((bf16[128,4,512]{2,1,0:T(4,128)(2,1)}), bf16[128,4,512]{2,1,0:T(4,128)(2,1)S(1)}, u32[]{:S(2)}, u32[]{:S(2)}) %all-to-all-start.1) | async-done | bytes 524320 | tf_op jit(solution)/shard_map/all_to_all | solution.py:54
  389.2 0.1 reshape.64
  389.3 0.8 convolution_multiply_fusion.1
  (13 shorter events, 0.1 us)
Async XLA Ops:
  7.2 1.5 copy-start.2
  7.2 302.6 %all-gather.2.cloned.1.call-start = ((), (), s32[]{:S(2)}) async-start(), calls=%async_computation.2 | async-start | bytes 50724864 | tf_op jit(solution)/shard_map/all_gather | solution.py:12
  9.4 28.5 %copy-start = (bf16[256,768]{1,0:T(8,128)(2,1)S(1)}, bf16[256,768]{1,0:T(8,128)(2,1)}, u32[]{:S(2)}) copy-start(bf16[256,768]{1,0:T(8,128)(2,1)} %param.5) | copy-start | bytes 1179652
  9.4 28.6 %copy-start.1 = (bf16[96,768]{1,0:T(8,128)(2,1)S(1)}, bf16[96,768]{1,0:T(8,128)(2,1)}, u32[]{:S(2)}) copy-start(bf16[96,768]{1,0:T(8,128)(2,1)} %param.6) | copy-start | bytes 442372
  21.2 337.1 %all-to-all-start = ((s32[128,1,4]{2,1,0:T(1,128)}), s32[128,1,4]{2,1,0:T(1,128)S(1)}, u32[]{:S(2)}, u32[]{:S(2)}) async-start(s32[128,1,4]{2,1,0:T(1,128)} %copy.15), calls=%async_computation | async-start | bytes 131072 | tf_op jit(solution)/shard_map/all_to_all | solution.py:55
  358.3 30.8 %all-to-all-start.1 = ((bf16[128,4,512]{2,1,0:T(4,128)(2,1)}), bf16[128,4,512]{2,1,0:T(4,128)(2,1)S(1)}, u32[]{:S(2)}, u32[]{:S(2)}) async-start(bf16[128,4,512]{2,1,0:T(4,128)(2,1)} %scatter_fusion.1), calls=%async_computation.1 | async-start | bytes 1048576 | tf_op jit(solution)/shard_map/all_to_all | solution.py:54
Sparse Core Ops, SparseCore 0:
  10.2 299.5 all-gather.1
